TPU v7x, 32 devices: a whole 2x2x4 slice. The times are simulated.
32 devices in a mesh: gx: 2 (over y), gy: 4 (over x, core), gz: 4 (over z).
Axes of the slice: x: 2, y: 2, z: 4, core: 2. Of those that a mesh axis runs over, the one named last changes fastest.
Arguments:
- positions: float32 [3, 8, 16, 512], P(None, 'gx', 'gy', 'gz'), may hold values from 0 to 1
- charges: float32 [8, 16, 512], P('gx', 'gy', 'gz'), may hold values from -1.2 to 1.2
- counts: int32 [8, 16, 16], P('gx', 'gy', 'gz'), may hold values from 16 to 32
- moment_shift: bfloat16 [8, 81, 81], replicated, may hold values from -0.25 to 0.25
- far_operators: bfloat16 [81, 25600], replicated, may hold values from -0.046875 to 0.046875
- local_shift: bfloat16 [8, 81, 81], replicated, may hold values from -0.625 to 0.625
- lattice_operator: bfloat16 [81, 81], replicated, may hold values from -0.625 to 0.625
Outputs:
- potential: float32 [8, 16, 512], P('gx', 'gy', 'gz')
- electric_field: float32 [3, 8, 16, 512], P(None, 'gx', 'gy', 'gz')
Inputs may be any that keep to these rules, and one draw needn't show every extreme that they name: `counts`: number of live charges in each leaf; slots at or past it are pads.
All inputs are finite; a program needn't handle non-finite values.
Results may differ from a plain program's by a relative error of at most 0.00035.
Values sent between devices are 32-bit elements; how exact they have to be, the bound alone decides.
A program may use at most 256 MiB of HBM per device.

v0:
```python
import jax
import jax.numpy as jnp
import numpy as np
from jax import lax
from jax.experimental import pallas as pl
from jax.experimental.pallas import tpu as pltpu
from jax.sharding import PartitionSpec as P

ORDER = 8
SLOTS = 32


SOFTENING = 0.0625


def padded(cells, sides, width):
    for axis, dim in sides:
        count = lax.axis_size(axis)
        head = lax.slice_in_dim(cells, 0, width, axis=dim)
        tail = lax.slice_in_dim(cells, cells.shape[dim] - width, cells.shape[dim], axis=dim)
        cells = jnp.concatenate(
            [
                lax.ppermute(tail, axis, [(i, (i + 1) % count) for i in range(count)]),
                cells,
                lax.ppermute(head, axis, [((i + 1) % count, i) for i in range(count)]),
            ],
            axis=dim,
        )
    return cells


def offset_table():
    listed = []
    for shift_x in range(-3, 4):
        for shift_y in range(-3, 4):
            for shift_z in range(-3, 4):
                if max(abs(shift_x), abs(shift_y), abs(shift_z)) >= 2:
                    listed.append((shift_x, shift_y, shift_z))
    return np.array(listed, dtype=np.int32)


def exponent_table(degree):
    listed = []
    for accumulated in range(degree + 1):
        for height in (0, 1):
            for power_x in range(accumulated - height + 1):
                listed.append((power_x, accumulated - height - power_x, height))
    return np.array(listed, dtype=np.int32)


NT = (((1,), (1,)), ((), ()))
TN = (((0,), (0,)), ((), ()))
F32 = jnp.float32
BF16 = jnp.bfloat16
LANES = 128


def split_rows(data):
    upper = data.astype(BF16)
    lower = (data - upper.astype(F32)).astype(BF16)
    return upper, lower


def apply(data, operator):
    upper, lower = split_rows(data)
    return lax.dot_general(upper, operator, NT, preferred_element_type=F32) + lax.dot_general(
        lower, operator, NT, preferred_element_type=F32
    )


def exact(left, right, dims):
    return lax.dot_general(
        left, right, dims, precision=lax.Precision.HIGHEST, preferred_element_type=F32
    )


def permutation(block_x, block_y, block_z):
    half_x, half_y, half_z = (block_x // 2, block_y // 2, block_z // 2)
    number = block_x * block_y * block_z
    table = np.zeros((number, number), np.float32)
    for x in range(block_x):
        for y in range(block_y):
            for z in range(block_z):
                octant = 4 * (x % 2) + 2 * (y % 2) + z % 2
                parent = (x // 2 * half_y + y // 2) * half_z + z // 2
                table[octant * (number // 8) + parent, (x * block_y + y) * block_z + z] = 1.0
    return table


def powers_of(values):
    listed = [jnp.ones_like(values)]
    for exponent in range(ORDER):
        listed.append(listed[-1] * values)
    return listed


def monomial_map(powers_x, powers_y, centred_z):
    made = {}
    for power_x, power_y, power_z in exponent_table(ORDER):
        key = (int(power_x), int(power_y), int(power_z))
        if key[2] == 0:
            made[key] = powers_x[key[0]] * powers_y[key[1]]
        else:
            made[key] = made[(key[0], key[1], 0)] * centred_z
    return made


def cell_picker(rows, cells):
    row = lax.broadcasted_iota(jnp.int32, (rows, cells * SLOTS), 0)
    lane = lax.broadcasted_iota(jnp.int32, (rows, cells * SLOTS), 1)
    return (lane // SLOTS == row).astype(F32)


def moment_kernel(cells, data_ref, shift_ref, order_ref, leaf_ref, mid_ref, upper_ref, table):
    terms = shift_ref.shape[1]
    columns = data_ref.shape[1]
    padded_terms = table.shape[0] // columns - 1
    powers_x = powers_of(data_ref[0] - 0.5)
    powers_x = [value * data_ref[3] for value in powers_x]
    powers_y = powers_of(data_ref[1] - 0.5)
    made = monomial_map(powers_x, powers_y, data_ref[2] - 0.5)
    for row, key in enumerate(exponent_table(ORDER)):
        table[row * columns : (row + 1) * columns, :] = made[tuple(int(v) for v in key)]
    spare = (padded_terms + 1 - terms) * columns
    table[terms * columns :, :] = jnp.zeros((spare, table.shape[1]), F32)
    picker = cell_picker(8, cells)
    leaf_ref[...] = jnp.zeros(leaf_ref.shape, F32)
    for column in range(columns):
        rows = table[pl.ds(column, padded_terms, stride=columns), :]
        found = exact(picker, rows, NT)
        leaf_ref[column * cells : (column + 1) * cells, :padded_terms] = found[:cells]
    ordered = exact(order_ref[...], leaf_ref[...], (((1,), (0,)), ((), ())))
    parents = ordered.shape[0] // 8
    mid = jnp.zeros((parents, terms), F32)
    for octant in range(8):
        piece = ordered[octant * parents : (octant + 1) * parents, :terms]
        mid = mid + apply(piece, shift_ref[octant])
    mid_ref[...] = jnp.zeros(mid_ref.shape, F32)
    mid_ref[:, :terms] = mid
    up = jnp.zeros((8, terms), F32)
    for octant in range(8):
        piece = jnp.broadcast_to(mid[octant : octant + 1], (8, terms))
        up = up + apply(piece, shift_ref[octant])
    upper_ref[...] = jnp.zeros(upper_ref.shape, F32)
    upper_ref[:, :terms] = up


def field_kernel(
    sizes,
    tops,
    plan_ref,
    where_ref,
    near_ref,
    live_ref,
    leaf_ref,
    mid_ref,
    upper_ref,
    root_ref,
    far_ref,
    down_ref,
    lattice_ref,
    order_ref,
    potential_ref,
    field_ref,
    spread,
    leaf_rows,
    mid_rows,
    operators,
    top_local,
    local_table,
    sums,
):
    block_x, block_y, block_z = sizes
    columns = block_x * block_y
    width = block_z * SLOTS
    terms = down_ref.shape[1]
    offsets = plan_ref.shape[0] // 16
    padded_terms = operators.shape[1]

    def fill(x, carry):
        for component in range(4):
            for move_z in range(3):
                for move_y in range(3):
                    spread[
                        (component * 3 + move_z) * 3 + move_y, pl.ds(x * block_y, block_y), :
                    ] = near_ref[
                        component, x, move_y : move_y + block_y, move_z * SLOTS : move_z * SLOTS + width
                    ]
        return carry

    lax.fori_loop(0, block_x + 2, fill, 0)

    def place(row, carry):
        start = row * terms
        base = jnp.minimum(start // LANES * LANES, far_ref.shape[1] - 2 * LANES)
        base = pl.multiple_of(base, LANES)
        held = far_ref[:, pl.ds(base, 2 * LANES)].astype(F32)
        held = jnp.concatenate(
            [held, jnp.zeros((padded_terms - terms, 2 * LANES), F32)], axis=0
        )
        turned = pltpu.roll(held, lax.rem(2 * LANES - (start - base), 2 * LANES), 1)
        return turned[:, :LANES].astype(BF16)

    def place_pair(pair, carry):
        operators[pair, :, :LANES] = place(2 * pair, carry)
        operators[pair, :, LANES:] = place(2 * pair + 1, carry)
        return carry

    lax.fori_loop(0, offsets // 2, place_pair, 0, unroll=2)

    lane = lax.broadcasted_iota(jnp.int32, (columns, width), 1)
    group = lane - lane % SLOTS
    turns = [group + (lane + step) % SLOTS for step in range(1, 5)]
    target_x = near_ref_target(near_ref, 0, sizes)
    target_y = near_ref_target(near_ref, 1, sizes)
    target_z = near_ref_target(near_ref, 2, sizes)

    def neighbour(which, totals):
        move_x = which // 9
        move_yz = which % 9
        move_y = move_yz // 3
        move_z = move_yz % 3
        slab = move_z * 3 + move_y
        rows = pl.ds(move_x * block_y, columns)
        shift_x = (move_x - 1).astype(F32)
        shift_y = (move_y - 1).astype(F32)
        shift_z = (move_z - 1).astype(F32)
        source = (
            spread[slab, rows, :] + shift_x,
            spread[9 + slab, rows, :] + shift_y,
            spread[18 + slab, rows, :] + shift_z,
            spread[27 + slab, rows, :],
        )
        own = which == 13

        def step(at, carry):
            held, totals = carry
            keep = jnp.where(own & (at == 0), 0.0, 1.0)
            sum_p, sum_x, sum_y, sum_z = totals
            for turn in range(4):
                if turn == 0:
                    s_x, s_y, s_z, s_q = held
                    s_q = s_q * keep
                else:
                    s_x, s_y, s_z, s_q = [
                        jnp.take_along_axis(value, turns[turn - 1], axis=1) for value in held
                    ]
                d_x = target_x - s_x
                d_y = target_y - s_y
                d_z = target_z - s_z
                inverse = lax.rsqrt(d_x * d_x + d_y * d_y + d_z * d_z + SOFTENING)
                weight = s_q * inverse
                sum_p = sum_p + weight
                cubic = weight * (inverse * inverse)
                sum_x = sum_x + cubic * d_x
                sum_y = sum_y + cubic * d_y
                sum_z = sum_z + cubic * d_z
            held = tuple(jnp.take_along_axis(value, turns[3], axis=1) for value in held)
            return held, (sum_p, sum_x, sum_y, sum_z)

        return lax.fori_loop(0, SLOTS // 4, step, (source, totals))[1]

    zero = jnp.zeros((columns, width), F32)
    near = lax.fori_loop(0, 27, neighbour, (zero, zero, zero, zero))

    row_of = lax.broadcasted_iota(jnp.int32, (8, LANES), 0)

    def sheets(held, cells, move):
        turned = pltpu.roll(held, (8 - (move + 2)) % 8, 0)
        if move == 3:
            turned = jnp.where(row_of % 2 == 0, turned, 0.0)
        if move == -3:
            turned = jnp.where(row_of % 2 == 1, turned, 0.0)
        upper = turned.astype(BF16).astype(F32)
        lower = pltpu.roll(turned - upper, cells, 0)
        made = jnp.where(row_of < cells, upper, lower)
        return jnp.where(row_of < 2 * cells, made, 0.0)

    wide_x, wide_y = leaf_ref.shape[0], leaf_ref.shape[1]
    leaf_rows[...] = jnp.zeros(leaf_rows.shape, F32)
    mid_rows[...] = jnp.zeros(mid_rows.shape, F32)

    def leaf_sheet(at, carry):
        x = at // wide_y
        y = at % wide_y
        held = leaf_ref[x, y]
        for move in range(-3, 4):
            leaf_rows[move + 3, x, y] = sheets(held, block_z, move)
        return carry

    lax.fori_loop(0, wide_x * wide_y, leaf_sheet, 0)
    mid_x, mid_y = mid_ref.shape[0], mid_ref.shape[1]

    def mid_sheet(at, carry):
        x = at // mid_y
        y = at % mid_y
        held = mid_ref[x, y]
        for move in range(-3, 4):
            mid_rows[move + 3, x, y] = sheets(held, block_z // 2, move)
        return carry

    lax.fori_loop(0, mid_x * mid_y, mid_sheet, 0)

    half_x, half_y = block_x // 2, block_y // 2
    upper_rows = upper_ref.shape[1]

    def gathered(row):
        at = row * 16
        move_z = plan_ref[at + 2]
        pieces = []
        for x in range(block_x):
            for y in range(block_y):
                pieces.append(leaf_rows[move_z, plan_ref[at + 4 + x % 2] + x, plan_ref[at + 6 + y % 2] + y])
        for x in range(half_x):
            for y in range(half_y):
                pieces.append(mid_rows[move_z, plan_ref[at + 8 + x % 2] + x, plan_ref[at + 10 + y % 2] + y])
        pieces.append(upper_ref[row, :, :LANES])
        pieces.append(upper_ref[row, :, LANES:])
        return jnp.concatenate(pieces, axis=0).astype(BF16)

    def far_step(pair, total):
        left = jnp.concatenate([gathered(2 * pair), gathered(2 * pair + 1)], axis=1)
        return total + lax.dot_general(left, operators[pair], NT, preferred_element_type=F32)

    leaf_count = columns * 8
    mid_count = half_x * half_y * 8
    total_rows = leaf_count + mid_count + 2 * upper_rows
    sums[...] = lax.fori_loop(
        0, offsets // 2, far_step, jnp.zeros((total_rows, padded_terms), F32), unroll=2
    )
    first = leaf_count + mid_count
    far_high = sums[first : first + upper_rows, :terms] + sums[first + upper_rows :, :terms]
    lattice = apply(jnp.broadcast_to(root_ref[...], (8, root_ref.shape[1]))[:, :terms], lattice_ref[...])
    top_local[...] = 0.125 * (far_high + lattice[:1])
    parent = top_local[pl.ds(where_ref[0] + 1, 1), :]
    upper = 0.25 * far_high[:1] + apply(jnp.broadcast_to(parent, (8, terms)), down_ref[where_ref[1]])[:1]
    upper = jnp.broadcast_to(upper, (8, terms))
    half_z = block_z // 2
    mids = jnp.concatenate([apply(upper, down_ref[octant])[:1] for octant in range(8)], axis=0)
    far_mids = []
    for column in range(half_x * half_y):
        held = sums[leaf_count + column * 8 : leaf_count + column * 8 + 8, :terms]
        far_mids.append(held[:half_z] + held[half_z : 2 * half_z])
    mids = mids + 0.5 * jnp.concatenate(far_mids, axis=0)
    pieces = [apply(mids, down_ref[octant]) for octant in range(8)]
    downs = exact(order_ref[...], jnp.concatenate(pieces, axis=0), TN)
    picker = cell_picker(block_z, block_z)
    for column in range(columns):
        held = sums[column * 8 : column * 8 + 8, :terms]
        local = held[:block_z] + held[block_z : 2 * block_z]
        local = local + downs[column * block_z : (column + 1) * block_z]
        local_table[pl.ds(column, terms, stride=columns), :] = exact(local, picker, TN)

    made = monomial_map(powers_of(target_x - 0.5), powers_of(target_y - 0.5), target_z - 0.5)
    out_p, out_x, out_y, out_z = near
    for row, key in enumerate(exponent_table(ORDER)):
        power_x, power_y, power_z = [int(v) for v in key]
        local = local_table[row * columns : (row + 1) * columns, :]
        out_p = out_p + local * made[(power_x, power_y, power_z)]
        if power_x:
            out_x = out_x - (float(power_x) * local) * made[(power_x - 1, power_y, power_z)]
        if power_y:
            out_y = out_y - (float(power_y) * local) * made[(power_x, power_y - 1, power_z)]
        if power_z:
            out_z = out_z - local * made[(power_x, power_y, 0)]
    live = live_ref[...]
    potential_ref[...] = out_p * live
    field_ref[0] = out_x * live
    field_ref[1] = out_y * live
    field_ref[2] = out_z * live


def near_ref_target(near_ref, component, sizes):
    block_x, block_y, block_z = sizes
    width = block_z * SLOTS
    return jnp.concatenate(
        [near_ref[component, 1 + x, 1 : 1 + block_y, SLOTS : SLOTS + width] for x in range(block_x)],
        axis=0,
    )


def plan_table(block_x, block_y):
    shifts = offset_table()
    plan = np.zeros((shifts.shape[0], 16), np.int32)
    for row, shift in enumerate(shifts):
        for axis in range(3):
            plan[row, axis] = shift[axis] + 3
        for axis in range(2):
            block = (block_x, block_y)[axis]
            for odd in range(2):
                admitted = -2 - odd <= shift[axis] <= 3 - odd
                plan[row, 4 + 2 * axis + odd] = shift[axis] + 2 if admitted else block + 4
                plan[row, 8 + 2 * axis + odd] = shift[axis] + 2 if admitted else block // 2 + 4
    return plan.reshape(-1)


def moments_merge(child, operators):
    size_x, size_y, size_z, terms = child.shape
    grouped = child.reshape(size_x // 2, 2, size_y // 2, 2, size_z // 2, 2, terms)
    grouped = grouped.transpose(0, 2, 4, 1, 3, 5, 6).reshape(-1, 8, terms)
    return jnp.einsum("pok,oak->pa", grouped, operators, precision=lax.Precision.HIGHEST)


def per_device(
    positions, charges, counts, moment_shift, far_operators, local_shift, lattice_operator
):
    block_x, block_y, column = charges.shape
    block_z = column // SLOTS
    sizes = (block_x, block_y, block_z)
    number_x = lax.axis_size("gx")
    number_y = lax.axis_size("gy")
    number_z = lax.axis_size("gz")
    index_x = lax.axis_index("gx")
    index_y = lax.axis_index("gy")
    index_z = lax.axis_index("gz")
    terms = moment_shift.shape[1]
    padded_terms = (terms + 15) // 16 * 16
    columns = block_x * block_y
    leaves = columns * block_z
    slot_of = jnp.arange(column, dtype=jnp.int32) % SLOTS
    live_mask = (slot_of[None, None, :] < jnp.repeat(counts, SLOTS, axis=2)).astype(F32)
    weights = charges * live_mask
    stacked = jnp.concatenate([positions, weights[None]], axis=0)
    column_halo = padded(stacked, (("gz", 3),), SLOTS)
    extended = padded(column_halo, (("gx", 1), ("gy", 2)), 1)
    order = jnp.asarray(permutation(*sizes))
    vmem = pl.BlockSpec(memory_space=pltpu.VMEM)
    smem = pl.BlockSpec(memory_space=pltpu.SMEM)
    leaf, mid, upper = pl.pallas_call(
        lambda *refs: moment_kernel(block_z, *refs),
        out_shape=(
            jax.ShapeDtypeStruct((leaves, LANES), F32),
            jax.ShapeDtypeStruct((leaves // 8, LANES), F32),
            jax.ShapeDtypeStruct((8, LANES), F32),
        ),
        in_specs=[vmem] * 3,
        out_specs=(vmem, vmem, vmem),
        scratch_shapes=[pltpu.VMEM(((padded_terms + 1) * columns, column), F32)],
        name="moments",
    )(stacked.reshape(4, columns, column), moment_shift, order)
    axes = (("gx", 0), ("gy", 1), ("gz", 2))
    wide_leaf = padded(leaf.reshape(block_x, block_y, block_z, LANES), axes, 2)
    wide_mid = padded(mid.reshape(block_x // 2, block_y // 2, block_z // 2, LANES), axes, 2)
    wide_mid = jnp.pad(wide_mid, ((0, 0), (0, 0), (0, 8 - wide_mid.shape[2]), (0, 0)))
    uppers = lax.all_gather(upper[:1], ("gx", "gy", "gz"), axis=0, tiled=True)
    tops = moments_merge(
        uppers[:, :terms].reshape(number_x, number_y, number_z, terms), moment_shift.astype(F32)
    )
    root = jnp.sum(tops, axis=0, keepdims=True)
    top_count = tops.shape[0]
    top_sizes = (number_x // 2, number_y // 2, number_z // 2)
    shifts = offset_table()
    offsets = shifts.shape[0]
    upper_rows = (1 + top_count + 7) // 8 * 8
    at = (index_x, index_y, index_z)
    numbers = (number_x, number_y, number_z)
    picked = 0
    admitted = True
    for axis in range(3):
        picked = picked * numbers[axis] + (at[axis] + shifts[:, axis]) % numbers[axis]
        odd = at[axis] % 2
        admitted = admitted & (shifts[:, axis] >= -2 - odd) & (shifts[:, axis] <= 3 - odd)
    picked = jnp.where(admitted, picked, -1)
    entries = number_x * number_y * number_z
    static = np.full((offsets, upper_rows), -1, np.int32)
    for row in range(offsets):
        for box in range(top_count):
            spot = (
                box // (top_sizes[1] * top_sizes[2]),
                box // top_sizes[2] % top_sizes[1],
                box % top_sizes[2],
            )
            moved = [(spot[axis] + int(shifts[row, axis])) % top_sizes[axis] for axis in range(3)]
            static[row, 1 + box] = (
                entries + (moved[0] * top_sizes[1] + moved[1]) * top_sizes[2] + moved[2]
            )
    index = jnp.where(jnp.arange(upper_rows)[None, :] == 0, picked[:, None], jnp.asarray(static))
    table = jnp.concatenate([uppers[:, :terms], tops], axis=0)
    table = jnp.pad(table, ((0, 0), (0, LANES - terms)))
    rounded = lax.reduce_precision(table, 8, 7)
    both = jnp.concatenate([rounded, lax.reduce_precision(table - rounded, 8, 7)], axis=1)
    chosen = (index[:, :, None] == jnp.arange(entries + top_count)[None, None, :]).astype(BF16)
    upper_table = jnp.dot(
        chosen.reshape(offsets * upper_rows, -1), both.astype(BF16), preferred_element_type=F32
    ).reshape(offsets, upper_rows, 2 * LANES)
    parent = (index_x // 2 * top_sizes[1] + index_y // 2) * top_sizes[2] + index_z // 2
    octant = index_x % 2 * 4 + index_y % 2 * 2 + index_z % 2
    where = jnp.stack([parent, octant]).astype(jnp.int32)
    wide_x, wide_y = block_x + 5, block_y + 5
    half_x, half_y = block_x // 2, block_y // 2
    potential, field_out = pl.pallas_call(
        lambda *refs: field_kernel(sizes, top_count, *refs),
        out_shape=(
            jax.ShapeDtypeStruct((columns, column), F32),
            jax.ShapeDtypeStruct((3, columns, column), F32),
        ),
        in_specs=[smem, smem] + [vmem] * 10,
        out_specs=(vmem, vmem),
        scratch_shapes=[
            pltpu.VMEM((36, (block_x + 4) * block_y, column), F32),
            pltpu.VMEM((7, block_x + 4 + block_x, block_y + 4 + block_y, 8, LANES), F32),
            pltpu.VMEM((7, half_x + 4 + half_x, half_y + 4 + half_y, 8, LANES), F32),
            pltpu.VMEM((offsets // 2, padded_terms, 2 * LANES), BF16),
            pltpu.VMEM((upper_rows, terms), F32),
            pltpu.VMEM(((padded_terms + 1) * columns, column), F32),
            pltpu.VMEM((columns * 8 + half_x * half_y * 8 + 2 * upper_rows, padded_terms), F32),
        ],
        compiler_params=pltpu.CompilerParams(vmem_limit_bytes=60 * 1024 * 1024),
        name="fields",
    )(
        jnp.asarray(plan_table(block_x, block_y)),
        where,
        extended,
        live_mask.reshape(columns, column),
        wide_leaf,
        wide_mid,
        upper_table,
        root,
        far_operators,
        local_shift,
        lattice_operator,
        order,
    )
    return (
        potential.reshape(block_x, block_y, column),
        field_out.reshape(3, block_x, block_y, column),
    )


def solution(mesh):
    placed = (
        P(None, "gx", "gy", "gz"),
        P("gx", "gy", "gz"),
        P("gx", "gy", "gz"),
        P(),
        P(),
        P(),
        P(),
    )
    return jax.shard_map(
        per_device,
        mesh=mesh,
        in_specs=placed,
        out_specs=(P("gx", "gy", "gz"), P(None, "gx", "gy", "gz")),
        check_vma=False,
    )
```

profile of v0, /device:TPU:0, one launch (start us, length us, event | category | flops | bytes accessed | tf_op | source)
XLA Modules:
  0.0 213.7 jit_solution(6860385271140741495)
XLA Ops:
  0.6 0.0 copy-start
  0.7 0.8 broadcast_in_dim.34
  1.5 0.1 reshape.61
  1.6 1.6 copy.26.refs_1_
  3.2 0.7 compare_select_fusion
  3.9 1.3 pad_maximum_fusion.6.refs_0_
  5.2 4.1 %moments.1 = (f32[64,128]{1,0:T(8,128)}, f32[8,128]{1,0:T(8,128)}, f32[8,128]{1,0:T(8,128)}) custom-call(f32[4,16,128]{2,1,0:T(8,128)} %pad_maximum_fusion.6.refs_0_, bf16[8,81,81]{2,1,0:T(8,128)(2,1)} %copy.26.refs_1_, f32[64,64]{1,0:T(8,128)} %constant.127.clone.refs_2_.refs_11_), custom_call_target="tpu_custom_call" | custom-call | tf_op jit(solution)/shard_map/moments/pallas_call | solution.py:429
  9.3 3.0 %collective-permute-start.12 = (f32[2,2,2,128]{3,2,1,0:T(2,128)}, f32[2,2,2,128]{3,2,1,0:T(2,128)S(1)}, u32[]{:S(2)}, u32[]{:S(2)}) collective-permute-start(f32[2,2,2,128]{3,2,1,0:T(2,128)} %bitcast.38), channel_id=1, source_target_pairs={{0,16},{16,0},{1,17},{17,1},{2,18},{18,2},{3,19},{19,3},{4,20},{20... | collective-permute-start | bytes 12296 | tf_op jit(solution)/shard_map/ppermute | solution.py:23
  12.3 0.1 collective-permute-start.13
  12.4 0.7 fusion.27
  13.1 2.0 collective-permute-start.6
  15.1 0.1 collective-permute-start.7
  15.1 0.9 slice_maximum_fusion
  16.0 2.1 collective-permute-start
  18.1 0.1 reshape.62
  18.2 0.7 slice_bitcast_fusion
  18.9 65.7 %all-gather = f32[32,1,128]{2,1,0:T(1,128)S(1)} all-gather(f32[1,1,128]{2,1,0:T(1,128)S(1)} %slice_bitcast_fusion), channel_id=1, replica_groups=mesh['gx'=2,'gy'=4,'gz'=4] {'gx','gy','gz'}, dimensions={0}, use_global_device_ids=true | all-gather | bytes 16896 | tf_op jit(solution)/shard_map/all_gather | solution.py:445
  84.6 1.7 fusion.28
  86.3 0.6 compare_convert_fusion.refs_3_
  86.9 0.7 fusion.19
  87.6 1.0 broadcast_select_fusion
  88.7 2.1 %fusion.refs_6_ = f32[316,8,256]{2,1,0:T(8,128)} fusion(s32[316,8]{1,0:T(8,128)S(1)} %broadcast_select_fusion, bf16[36,128]{1,0:T(8,128)(2,1)S(1)} %get-tuple-element.25, bf16[36,128]{1,0:T(8,128)(2,1)S(1)} %get-tuple-element.24), kind=kOutput, calls=%fused_computation.1 | convolution fusion | flops 46723968 | bytes 2617216 | tf_op jit(solution)/shard_map/dot_general | solution.py:483
  90.8 0.6 pad_add_fusion.refs_1_
  91.5 0.7 copy.29.refs_9_
  92.2 0.0 collective-permute-start.1
  92.2 0.1 collective-permute-start.14
  92.3 1.7 collective-permute-start.15
  94.0 2.1 collective-permute-done.1
  96.1 0.1 pad_maximum_fusion.16
  96.2 0.9 collective-permute-start.2
  97.0 1.2 collective-permute-start.3
  98.3 0.1 collective-permute-start.16
  98.4 3.8 %collective-permute-start.17 = (f32[6,6,2,128]{3,2,1,0:T(2,128)S(1)}, f32[6,6,2,128]{3,2,1,0:T(2,128)S(1)}, u32[]{:S(2)}, u32[]{:S(2)}) collective-permute-start(f32[6,6,2,128]{3,2,1,0:T(2,128)S(1)} %pad_maximum_fusion.4), channel_id=1, source_target_pairs={{1,0},{2,1},{3,2},{0,3},{5,4},{6,5},{7,6},{4,7},{9,8},{10,9},{11,1... | collective-permute-start | bytes 110600 | tf_op jit(solution)/shard_map/ppermute | solution.py:25
  102.2 0.2 pad_maximum_fusion.12
  102.4 0.1 collective-permute-start.4
  102.5 1.7 collective-permute-start.5
  104.2 1.5 collective-permute-done.4
  105.7 0.2 collective-permute-start.9
  106.0 0.8 pad_maximum_fusion.1.refs_2_
  106.8 0.8 collective-permute-done.8
  107.5 0.0 collective-permute-done.9
  107.6 0.1 fusion.25
  107.6 0.1 collective-permute-start.10
  107.7 3.8 %collective-permute-start.11 = (f32[8,8,2,128]{3,2,1,0:T(2,128)S(1)}, f32[8,8,2,128]{3,2,1,0:T(2,128)S(1)}, u32[]{:S(2)}, u32[]{:S(2)}) collective-permute-start(f32[8,8,2,128]{3,2,1,0:T(2,128)S(1)} %get-tuple-element.13), channel_id=1, source_target_pairs={{1,0},{2,1},{3,2},{0,3},{5,4},{6,5},{7,6},{4,7},{9,8},{10,9},{11,1... | collective-permute-start | bytes 196616 | tf_op jit(solution)/shard_map/ppermute | solution.py:25
  111.5 0.7 select_maximum_fusion.refs_5_
  112.3 1.5 collective-permute-done.10
  113.8 0.8 pad_maximum_fusion.refs_4_
  114.6 99.1 %fields.1 = (f32[16,128]{1,0:T(8,128)}, f32[3,16,128]{2,1,0:T(8,128)}) custom-call(s32[5056]{0:T(1024)} %constant.132.clone.refs_0_, s32[2]{0:T(128)} %pad_add_fusion.refs_1_, f32[4,6,6,192]{3,2,1,0:T(8,128)} %pad_maximum_fusion.1.refs_2_, f32[16,128]{1,0:T(8,128)} %compare_convert_fusion.refs_3_, f32[8,8,8,128]{3,2,1,0:T(8,128)} %pad_maximum_fusion.refs_4_, ...), custom_call_target="tpu_custom_call" | custom-call | tf_op jit(solution)/shard_map/fields/pallas_call | solution.py:491
  (30 shorter events, 0.2 us)
Async XLA Ops:
  0.6 95.4 %copy-start = (f32[3,4,4,128]{3,2,1,0:T(4,128)S(1)}, f32[3,4,4,128]{3,2,1,0:T(4,128)}, u32[]{:S(2)}) copy-start(f32[3,4,4,128]{3,2,1,0:T(4,128)} %param.19) | copy-start | bytes 73732
  0.6 90.8 %copy-start.2 = (bf16[8,81,81]{2,0,1:T(8,128)(2,1)S(1)}, bf16[8,81,81]{2,0,1:T(8,128)(2,1)}, u32[]{:S(2)}) copy-start(bf16[8,81,81]{2,0,1:T(8,128)(2,1)} %param.24) | copy-start | bytes 314932
  9.3 82.8 %copy-start.3 = (f32[8,128]{1,0:T(8,128)S(1)}, f32[8,128]{1,0:T(8,128)}, u32[]{:S(2)}) copy-start(f32[8,128]{1,0:T(8,128)} %get-tuple-element.8) | copy-start | bytes 12292
  9.3 92.9 %copy-start.1 = (f32[64,128]{1,0:T(8,128)S(1)}, f32[64,128]{1,0:T(8,128)}, u32[]{:S(2)}) copy-start(f32[64,128]{1,0:T(8,128)} %get-tuple-element.7) | copy-start | bytes 98308
  9.3 82.8 %collective-permute-start.12 = (f32[2,2,2,128]{3,2,1,0:T(2,128)}, f32[2,2,2,128]{3,2,1,0:T(2,128)S(1)}, u32[]{:S(2)}, u32[]{:S(2)}) collective-permute-start(f32[2,2,2,128]{3,2,1,0:T(2,128)} %bitcast.38), channel_id=1, source_target_pairs={{0,16},{16,0},{1,17},{17,1},{2,18},{18,2},{3,19},{19,3},{4,20},{20... | collective-permute-start | bytes 12296 | tf_op jit(solution)/shard_map/ppermute | solution.py:23
  12.3 79.8 %collective-permute-start.13 = (f32[2,2,2,128]{3,2,1,0:T(2,128)}, f32[2,2,2,128]{3,2,1,0:T(2,128)S(1)}, u32[]{:S(2)}, u32[]{:S(2)}) collective-permute-start(f32[2,2,2,128]{3,2,1,0:T(2,128)} %bitcast.39), channel_id=1, source_target_pairs={{16,0},{0,16},{17,1},{1,17},{18,2},{2,18},{19,3},{3,19},{20,4},{4,... | collective-permute-start | bytes 12296 | tf_op jit(solution)/shard_map/ppermute | solution.py:25
  13.1 85.2 %collective-permute-start.6 = (f32[2,4,4,128]{3,2,1,0:T(4,128)S(1)}, f32[2,4,4,128]{3,2,1,0:T(4,128)S(1)}, u32[]{:S(2)}, u32[]{:S(2)}) collective-permute-start(f32[2,4,4,128]{3,2,1,0:T(4,128)S(1)} %bitcast.44), channel_id=1, source_target_pairs={{0,16},{16,0},{1,17},{17,1},{2,18},{18,2},{3,19},{19,3},{4,20},{20... | collective-permute-start | bytes 49160 | tf_op jit(solution)/shard_map/ppermute | solution.py:23
  15.1 87.1 %collective-permute-start.7 = (f32[2,4,4,128]{3,2,1,0:T(4,128)S(1)}, f32[2,4,4,128]{3,2,1,0:T(4,128)S(1)}, u32[]{:S(2)}, u32[]{:S(2)}) collective-permute-start(f32[2,4,4,128]{3,2,1,0:T(4,128)S(1)} %bitcast.43), channel_id=1, source_target_pairs={{16,0},{0,16},{17,1},{1,17},{18,2},{2,18},{19,3},{3,19},{20,4},{4,... | collective-permute-start | bytes 49160 | tf_op jit(solution)/shard_map/ppermute | solution.py:25
  16.0 76.2 %collective-permute-start = (f32[4,4,4,32]{3,2,1,0:T(4,128)S(1)}, f32[4,4,4,32]{3,2,1,0:T(4,128)S(1)}, u32[]{:S(2)}, u32[]{:S(2)}) collective-permute-start(f32[4,4,4,32]{3,2,1,0:T(4,128)S(1)} %get-tuple-element.22), channel_id=1, source_target_pairs={{0,1},{1,2},{2,3},{3,0},{4,5},{5,6},{6,7},{7,4},{8,9},{9,10},{10,1... | collective-permute-start | bytes 24584 | tf_op jit(solution)/shard_map/ppermute | solution.py:23
  92.2 3.9 %collective-permute-start.1 = (f32[4,4,4,32]{3,2,1,0:T(4,128)S(1)}, f32[4,4,4,32]{3,2,1,0:T(4,128)S(1)}, u32[]{:S(2)}, u32[]{:S(2)}) collective-permute-start(f32[4,4,4,32]{3,2,1,0:T(4,128)S(1)} %get-tuple-element.23), channel_id=1, source_target_pairs={{1,0},{2,1},{3,2},{0,3},{5,4},{6,5},{7,6},{4,7},{9,8},{10,9},{11,1... | collective-permute-start | bytes 24584 | tf_op jit(solution)/shard_map/ppermute | solution.py:25
  92.2 4.9 %collective-permute-start.14 = (f32[6,2,2,128]{3,2,1,0:T(2,128)S(1)}, f32[6,2,2,128]{3,2,1,0:T(2,128)S(1)}, u32[]{:S(2)}, u32[]{:S(2)}) collective-permute-start(f32[6,2,2,128]{3,2,1,0:T(2,128)S(1)} %pad_maximum_fusion.17), channel_id=1, source_target_pairs={{0,4},{4,8},{8,12},{12,0},{1,5},{5,9},{9,13},{13,1},{2,6},{6,10},{... | collective-permute-start | bytes 36872 | tf_op jit(solution)/shard_map/ppermute | solution.py:23
  92.3 6.0 %collective-permute-start.15 = (f32[6,2,2,128]{3,2,1,0:T(2,128)S(1)}, f32[6,2,2,128]{3,2,1,0:T(2,128)S(1)}, u32[]{:S(2)}, u32[]{:S(2)}) collective-permute-start(f32[6,2,2,128]{3,2,1,0:T(2,128)S(1)} %pad_maximum_fusion.17), channel_id=1, source_target_pairs={{4,0},{8,4},{12,8},{0,12},{5,1},{9,5},{13,9},{1,13},{6,2},{10,6},{... | collective-permute-start | bytes 36872 | tf_op jit(solution)/shard_map/ppermute | solution.py:25
  96.2 6.0 %collective-permute-start.2 = (f32[4,1,4,192]{3,2,1,0:T(4,128)S(1)}, f32[4,1,4,192]{3,2,1,0:T(4,128)S(1)}, u32[]{:S(2)}, u32[]{:S(2)}) collective-permute-start(f32[4,1,4,192]{3,2,1,0:T(4,128)S(1)} %get-tuple-element.16), channel_id=1, source_target_pairs={{0,16},{16,0},{1,17},{17,1},{2,18},{18,2},{3,19},{19,3},{4,20},{20... | collective-permute-start | bytes 36872 | tf_op jit(solution)/shard_map/ppermute | solution.py:23
  97.0 5.2 %collective-permute-start.3 = (f32[4,1,4,192]{3,2,1,0:T(4,128)S(1)}, f32[4,1,4,192]{3,2,1,0:T(4,128)S(1)}, u32[]{:S(2)}, u32[]{:S(2)}) collective-permute-start(f32[4,1,4,192]{3,2,1,0:T(4,128)S(1)} %get-tuple-element.17), channel_id=1, source_target_pairs={{16,0},{0,16},{17,1},{1,17},{18,2},{2,18},{19,3},{3,19},{20,4},{4,... | collective-permute-start | bytes 36872 | tf_op jit(solution)/shard_map/ppermute | solution.py:25
  98.3 13.2 %collective-permute-start.16 = (f32[6,6,2,128]{3,2,1,0:T(2,128)S(1)}, f32[6,6,2,128]{3,2,1,0:T(2,128)S(1)}, u32[]{:S(2)}, u32[]{:S(2)}) collective-permute-start(f32[6,6,2,128]{3,2,1,0:T(2,128)S(1)} %pad_maximum_fusion.4), channel_id=1, source_target_pairs={{0,1},{1,2},{2,3},{3,0},{4,5},{5,6},{6,7},{7,4},{8,9},{9,10},{10,1... | collective-permute-start | bytes 110600 | tf_op jit(solution)/shard_map/ppermute | solution.py:23
  98.4 13.2 %collective-permute-start.17 = (f32[6,6,2,128]{3,2,1,0:T(2,128)S(1)}, f32[6,6,2,128]{3,2,1,0:T(2,128)S(1)}, u32[]{:S(2)}, u32[]{:S(2)}) collective-permute-start(f32[6,6,2,128]{3,2,1,0:T(2,128)S(1)} %pad_maximum_fusion.4), channel_id=1, source_target_pairs={{1,0},{2,1},{3,2},{0,3},{5,4},{6,5},{7,6},{4,7},{9,8},{10,9},{11,1... | collective-permute-start | bytes 110600 | tf_op jit(solution)/shard_map/ppermute | solution.py:25
  102.4 3.3 %collective-permute-start.4 = (f32[4,6,1,192]{3,2,1,0:T(1,128)S(1)}, f32[4,6,1,192]{3,2,1,0:T(1,128)S(1)}, u32[]{:S(2)}, u32[]{:S(2)}) collective-permute-start(f32[4,6,1,192]{3,2,1,0:T(1,128)S(1)} %get-tuple-element.14), channel_id=1, source_target_pairs={{0,4},{4,8},{8,12},{12,0},{1,5},{5,9},{9,13},{13,1},{2,6},{6,10},{... | collective-permute-start | bytes 55304 | tf_op jit(solution)/shard_map/ppermute | solution.py:23
  102.5 3.5 %collective-permute-start.5 = (f32[4,6,1,192]{3,2,1,0:T(1,128)S(1)}, f32[4,6,1,192]{3,2,1,0:T(1,128)S(1)}, u32[]{:S(2)}, u32[]{:S(2)}) collective-permute-start(f32[4,6,1,192]{3,2,1,0:T(1,128)S(1)} %get-tuple-element.15), channel_id=1, source_target_pairs={{4,0},{8,4},{12,8},{0,12},{5,1},{9,5},{13,9},{1,13},{6,2},{10,6},{... | collective-permute-start | bytes 55304 | tf_op jit(solution)/shard_map/ppermute | solution.py:25
  104.2 3.3 %collective-permute-start.8 = (f32[8,2,4,128]{3,2,1,0:T(4,128)S(1)}, f32[8,2,4,128]{3,2,1,0:T(4,128)S(1)}, u32[]{:S(2)}, u32[]{:S(2)}) collective-permute-start(f32[8,2,4,128]{3,2,1,0:T(4,128)S(1)} %get-tuple-element.18), channel_id=1, source_target_pairs={{0,4},{4,8},{8,12},{12,0},{1,5},{5,9},{9,13},{13,1},{2,6},{6,10},{... | collective-permute-start | bytes 98312 | tf_op jit(solution)/shard_map/ppermute | solution.py:23
  105.7 1.8 collective-permute-start.9
  107.6 6.1 %collective-permute-start.10 = (f32[8,8,2,128]{3,2,1,0:T(2,128)S(1)}, f32[8,8,2,128]{3,2,1,0:T(2,128)S(1)}, u32[]{:S(2)}, u32[]{:S(2)}) collective-permute-start(f32[8,8,2,128]{3,2,1,0:T(2,128)S(1)} %get-tuple-element.12), channel_id=1, source_target_pairs={{0,1},{1,2},{2,3},{3,0},{4,5},{5,6},{6,7},{7,4},{8,9},{9,10},{10,1... | collective-permute-start | bytes 196616 | tf_op jit(solution)/shard_map/ppermute | solution.py:23
  107.7 6.1 %collective-permute-start.11 = (f32[8,8,2,128]{3,2,1,0:T(2,128)S(1)}, f32[8,8,2,128]{3,2,1,0:T(2,128)S(1)}, u32[]{:S(2)}, u32[]{:S(2)}) collective-permute-start(f32[8,8,2,128]{3,2,1,0:T(2,128)S(1)} %get-tuple-element.13), channel_id=1, source_target_pairs={{1,0},{2,1},{3,2},{0,3},{5,4},{6,5},{7,6},{4,7},{9,8},{10,9},{11,1... | collective-permute-start | bytes 196616 | tf_op jit(solution)/shard_map/ppermute | solution.py:25
where the time goes:
time: 214 us
  Pallas kernels  103 us (48%)
  blocking collectives  65.7 us (31%)
  starting transfers between devices  20.8 us (10%)
  other arithmetic  8.63 us (4%)
  waiting for transfers between devices  5.89 us (3%)
  local copies, waits for them, and re-layouts  4.82 us (2%)
  matrix products  3.82 us (2%)
    pallas_call x1, Pallas kernels, per_device(): pl.pallas_call(lambda *refs: field_kernel(sizes, top_count, *refs), out_s...  99.1 us
    all_gather x1, blocking collectives, per_device(): uppers = lax.all_gather(upper[:1], ('gx', 'gy', 'gz'), axis=0, tiled=True)  65.7 us
    ppermute x9, starting transfers between devices, padded(): lax.ppermute(head, axis, [((i + 1) % count, i) for i in range(count)])  12.7 us
    ppermute x9, starting transfers between devices, padded(): lax.ppermute(tail, axis, [(i, (i + 1) % count) for i in range(count)])  8.13 us
  transfers between devices with their start and end apart: 18, of which 4 were waited for; matrix products, arithmetic and copies ran while one was open for 6% of the time, Pallas kernels for 0%

commit v1 on v0

--- a/solution.py
+++ b/solution.py
@@ -111,7 +111,40 @@
     return (lane // SLOTS == row).astype(F32)
 
 
-def moment_kernel(cells, data_ref, shift_ref, order_ref, leaf_ref, mid_ref, upper_ref, table):
+def halo_slices(move, block, halo):
+    if move == 1:
+        return pl.ds(block, halo), pl.ds(0, halo)
+    if move == -1:
+        return pl.ds(halo, halo), pl.ds(block + halo, halo)
+    return pl.ds(halo, block), pl.ds(halo, block)
+
+
+def halo_copies(window, block, halo, numbers, at, sends, receives):
+    copies = []
+    for count in range(27):
+        moves = (count // 9 - 1, count // 3 % 3 - 1, count % 3 - 1)
+        if moves == (0, 0, 0):
+            continue
+        target = tuple(
+            lax.rem(at[axis] + moves[axis] + numbers[axis], numbers[axis]) for axis in range(3)
+        )
+        from_x, to_x = halo_slices(moves[0], block[0], halo)
+        from_y, to_y = halo_slices(moves[1], block[1], halo)
+        copies.append(
+            pltpu.make_async_remote_copy(
+                src_ref=window.at[1, from_x, from_y],
+                dst_ref=window.at[1 - moves[2], to_x, to_y],
+                send_sem=sends.at[count],
+                recv_sem=receives.at[count],
+                device_id=target,
+                device_id_type=pl.DeviceIdType.MESH,
+            )
+        )
+    return copies
+
+
+def local_moments(sizes, data_ref, shift_ref, order_ref, table, leaf_flat, leaf_wide, mid_wide, own_upper):
+    block_x, block_y, cells = sizes
     terms = shift_ref.shape[1]
     columns = data_ref.shape[1]
     padded_terms = table.shape[0] // columns - 1
@@ -124,44 +157,55 @@
     spare = (padded_terms + 1 - terms) * columns
     table[terms * columns :, :] = jnp.zeros((spare, table.shape[1]), F32)
     picker = cell_picker(8, cells)
-    leaf_ref[...] = jnp.zeros(leaf_ref.shape, F32)
     for column in range(columns):
         rows = table[pl.ds(column, padded_terms, stride=columns), :]
-        found = exact(picker, rows, NT)
-        leaf_ref[column * cells : (column + 1) * cells, :padded_terms] = found[:cells]
-    ordered = exact(order_ref[...], leaf_ref[...], (((1,), (0,)), ((), ())))
+        found = exact(picker, rows, NT)[:cells]
+        found = jnp.concatenate([found, jnp.zeros((cells, LANES - padded_terms), F32)], axis=1)
+        leaf_flat[column * cells : (column + 1) * cells, :] = found
+        leaf_wide[1, 2 + column // block_y, 2 + column % block_y] = found
+    ordered = exact(order_ref[...], leaf_flat[...], (((1,), (0,)), ((), ())))
     parents = ordered.shape[0] // 8
     mid = jnp.zeros((parents, terms), F32)
     for octant in range(8):
         piece = ordered[octant * parents : (octant + 1) * parents, :terms]
         mid = mid + apply(piece, shift_ref[octant])
-    mid_ref[...] = jnp.zeros(mid_ref.shape, F32)
-    mid_ref[:, :terms] = mid
+    spare_lanes = jnp.zeros((8, LANES - terms), F32)
+    mids = jnp.concatenate([mid, spare_lanes], axis=1)
+    half_y, half_z = block_y // 2, cells // 2
+    for column in range(block_x // 2 * half_y):
+        mid_wide[1, 2 + column // half_y, 2 + column % half_y] = mids[
+            column * half_z : (column + 1) * half_z
+        ]
     up = jnp.zeros((8, terms), F32)
     for octant in range(8):
         piece = jnp.broadcast_to(mid[octant : octant + 1], (8, terms))
         up = up + apply(piece, shift_ref[octant])
-    upper_ref[...] = jnp.zeros(upper_ref.shape, F32)
-    upper_ref[:, :terms] = up
+    own_upper[...] = jnp.concatenate([up, spare_lanes], axis=1)
 
 
 def field_kernel(
     sizes,
-    tops,
+    numbers,
     plan_ref,
     where_ref,
-    near_ref,
+    own_ref,
+    data_ref,
     live_ref,
-    leaf_ref,
-    mid_ref,
-    upper_ref,
-    root_ref,
+    shift_ref,
     far_ref,
     down_ref,
     lattice_ref,
     order_ref,
+    merge_ref,
+    chosen_ref,
     potential_ref,
     field_ref,
+    near_wide,
+    leaf_wide,
+    mid_wide,
+    uppers,
+    leaf_flat,
+    upper_rows_ref,
     spread,
     leaf_rows,
     mid_rows,
@@ -169,6 +213,10 @@
     top_local,
     local_table,
     sums,
+    sends,
+    receives,
+    upper_send,
+    upper_receive,
 ):
     block_x, block_y, block_z = sizes
     columns = block_x * block_y
@@ -177,18 +225,59 @@
     offsets = plan_ref.shape[0] // 16
     padded_terms = operators.shape[1]
 
-    def fill(x, carry):
-        for component in range(4):
-            for move_z in range(3):
-                for move_y in range(3):
-                    spread[
-                        (component * 3 + move_z) * 3 + move_y, pl.ds(x * block_y, block_y), :
-                    ] = near_ref[
-                        component, x, move_y : move_y + block_y, move_z * SLOTS : move_z * SLOTS + width
-                    ]
-        return carry
-
-    lax.fori_loop(0, block_x + 2, fill, 0)
+    at = tuple(lax.axis_index(axis) for axis in ("gx", "gy", "gz"))
+    devices = numbers[0] * numbers[1] * numbers[2]
+    rank = (at[0] * numbers[1] + at[1]) * numbers[2] + at[2]
+
+    def coordinates(step):
+        other = lax.rem(rank + step, devices)
+        return (
+            other // (numbers[1] * numbers[2]),
+            lax.rem(other // numbers[2], numbers[1]),
+            lax.rem(other, numbers[2]),
+        )
+
+    barrier = pltpu.get_barrier_semaphore()
+
+    def greet(step, carry):
+        pl.semaphore_signal(
+            barrier, inc=1, device_id=coordinates(step), device_id_type=pl.DeviceIdType.MESH
+        )
+        return carry
+
+    lax.fori_loop(1, devices, greet, 0)
+    near_wide[1, 1 : 1 + block_x, 1 : 1 + block_y] = own_ref[...]
+    own_slot = uppers.at[pl.ds(pl.multiple_of(rank * 8, 8), 8)]
+    local_moments(
+        sizes, data_ref, shift_ref, order_ref, local_table, leaf_flat, leaf_wide, mid_wide, own_slot
+    )
+    halves = (block_x // 2, block_y // 2)
+    near_copies = halo_copies(near_wide, sizes, 1, numbers, at, sends.at[0], receives.at[0])
+    leaf_copies = halo_copies(leaf_wide, sizes, 2, numbers, at, sends.at[1], receives.at[1])
+    mid_copies = halo_copies(mid_wide, halves, 2, numbers, at, sends.at[2], receives.at[2])
+
+    def upper_copy(step):
+        return pltpu.make_async_remote_copy(
+            src_ref=own_slot,
+            dst_ref=own_slot,
+            send_sem=upper_send.at[step],
+            recv_sem=upper_receive.at[step],
+            device_id=coordinates(step),
+            device_id_type=pl.DeviceIdType.MESH,
+        )
+
+    def send_upper(step, carry):
+        upper_copy(step).start()
+        return carry
+
+    def wait_upper(step, carry):
+        upper_copy(step).wait()
+        return carry
+
+    pl.semaphore_wait(barrier, devices - 1)
+    for copy in near_copies + leaf_copies + mid_copies:
+        copy.start()
+    lax.fori_loop(1, devices, send_upper, 0)
 
     def place(row, carry):
         start = row * terms
@@ -211,9 +300,33 @@
     lane = lax.broadcasted_iota(jnp.int32, (columns, width), 1)
     group = lane - lane % SLOTS
     turns = [group + (lane + step) % SLOTS for step in range(1, 5)]
-    target_x = near_ref_target(near_ref, 0, sizes)
-    target_y = near_ref_target(near_ref, 1, sizes)
-    target_z = near_ref_target(near_ref, 2, sizes)
+    target_x = data_ref[0]
+    target_y = data_ref[1]
+    target_z = data_ref[2]
+    for copy in near_copies:
+        copy.wait()
+
+    def fill(x, carry):
+        for y in range(block_y + 2):
+            low, own, high = (near_wide[0, x, y], near_wide[1, x, y], near_wide[2, x, y])
+            moved = (
+                jnp.concatenate([low[:, width - SLOTS :], own[:, : width - SLOTS]], axis=1),
+                own,
+                jnp.concatenate([own[:, SLOTS:], high[:, :SLOTS]], axis=1),
+            )
+            for move_y in range(3):
+                if not 0 <= y - move_y < block_y:
+                    continue
+                for move_z in range(3):
+                    for component in range(4):
+                        spread[
+                            (component * 3 + move_z) * 3 + move_y,
+                            pl.ds(x * block_y + y - move_y, 1),
+                            :,
+                        ] = moved[move_z][component : component + 1]
+        return carry
+
+    lax.fori_loop(0, block_x + 2, fill, 0)
 
     def neighbour(which, totals):
         move_x = which // 9
@@ -276,25 +389,33 @@
         made = jnp.where(row_of < cells, upper, lower)
         return jnp.where(row_of < 2 * cells, made, 0.0)
 
-    wide_x, wide_y = leaf_ref.shape[0], leaf_ref.shape[1]
+    for copy in leaf_copies + mid_copies:
+        copy.wait()
+    lax.fori_loop(1, devices, wait_upper, 0)
+    wide_x, wide_y = leaf_wide.shape[1], leaf_wide.shape[2]
     leaf_rows[...] = jnp.zeros(leaf_rows.shape, F32)
     mid_rows[...] = jnp.zeros(mid_rows.shape, F32)
 
     def leaf_sheet(at, carry):
         x = at // wide_y
         y = at % wide_y
-        held = leaf_ref[x, y]
+        held = jnp.concatenate(
+            [leaf_wide[0, x, y][block_z - 2 :], leaf_wide[1, x, y], leaf_wide[2, x, y][:2]], axis=0
+        )
         for move in range(-3, 4):
             leaf_rows[move + 3, x, y] = sheets(held, block_z, move)
         return carry
 
     lax.fori_loop(0, wide_x * wide_y, leaf_sheet, 0)
-    mid_x, mid_y = mid_ref.shape[0], mid_ref.shape[1]
+    mid_x, mid_y = mid_wide.shape[1], mid_wide.shape[2]
 
     def mid_sheet(at, carry):
         x = at // mid_y
         y = at % mid_y
-        held = mid_ref[x, y]
+        held = jnp.concatenate(
+            [mid_wide[0, x, y], mid_wide[1, x, y], mid_wide[2, x, y], jnp.zeros((2, LANES), F32)],
+            axis=0,
+        )
         for move in range(-3, 4):
             mid_rows[move + 3, x, y] = sheets(held, block_z // 2, move)
         return carry
@@ -302,7 +423,27 @@
     lax.fori_loop(0, mid_x * mid_y, mid_sheet, 0)
 
     half_x, half_y = block_x // 2, block_y // 2
-    upper_rows = upper_ref.shape[1]
+    upper_rows = chosen_ref.shape[1]
+    all_upper = uppers[pl.ds(0, devices, stride=8), :]
+    sorted_upper = exact(merge_ref[...], all_upper, (((1,), (0,)), ((), ())))
+    tops = devices // 8
+    merged = jnp.zeros((tops, terms), F32)
+    for octant in range(8):
+        merged = merged + apply(sorted_upper[octant * tops : (octant + 1) * tops, :terms], shift_ref[octant])
+    root = jnp.sum(merged, axis=0, keepdims=True)
+    merged = jnp.concatenate([merged, jnp.zeros((tops, LANES - terms), F32)], axis=1)
+    both = jnp.concatenate(split_rows(jnp.concatenate([all_upper, merged], axis=0)), axis=1)
+
+    def pick(group, carry):
+        found = jnp.dot(
+            chosen_ref[pl.ds(group * 4, 4)].reshape(4 * upper_rows, -1).astype(BF16),
+            both,
+            preferred_element_type=F32,
+        )
+        upper_rows_ref[pl.ds(group * 4, 4)] = found.reshape(4, upper_rows, 2 * LANES)
+        return carry
+
+    lax.fori_loop(0, offsets // 4, pick, 0)
 
     def gathered(row):
         at = row * 16
@@ -314,8 +455,8 @@
         for x in range(half_x):
             for y in range(half_y):
                 pieces.append(mid_rows[move_z, plan_ref[at + 8 + x % 2] + x, plan_ref[at + 10 + y % 2] + y])
-        pieces.append(upper_ref[row, :, :LANES])
-        pieces.append(upper_ref[row, :, LANES:])
+        pieces.append(upper_rows_ref[row, :, :LANES])
+        pieces.append(upper_rows_ref[row, :, LANES:])
         return jnp.concatenate(pieces, axis=0).astype(BF16)
 
     def far_step(pair, total):
@@ -330,7 +471,7 @@
     )
     first = leaf_count + mid_count
     far_high = sums[first : first + upper_rows, :terms] + sums[first + upper_rows :, :terms]
-    lattice = apply(jnp.broadcast_to(root_ref[...], (8, root_ref.shape[1]))[:, :terms], lattice_ref[...])
+    lattice = apply(jnp.broadcast_to(root, (8, terms)), lattice_ref[...])
     top_local[...] = 0.125 * (far_high + lattice[:1])
     parent = top_local[pl.ds(where_ref[0] + 1, 1), :]
     upper = 0.25 * far_high[:1] + apply(jnp.broadcast_to(parent, (8, terms)), down_ref[where_ref[1]])[:1]
@@ -370,15 +511,6 @@
     field_ref[2] = out_z * live
 
 
-def near_ref_target(near_ref, component, sizes):
-    block_x, block_y, block_z = sizes
-    width = block_z * SLOTS
-    return jnp.concatenate(
-        [near_ref[component, 1 + x, 1 : 1 + block_y, SLOTS : SLOTS + width] for x in range(block_x)],
-        axis=0,
-    )
-
-
 def plan_table(block_x, block_y):
     shifts = offset_table()
     plan = np.zeros((shifts.shape[0], 16), np.int32)
@@ -392,13 +524,6 @@
                 plan[row, 4 + 2 * axis + odd] = shift[axis] + 2 if admitted else block + 4
                 plan[row, 8 + 2 * axis + odd] = shift[axis] + 2 if admitted else block // 2 + 4
     return plan.reshape(-1)
-
-
-def moments_merge(child, operators):
-    size_x, size_y, size_z, terms = child.shape
-    grouped = child.reshape(size_x // 2, 2, size_y // 2, 2, size_z // 2, 2, terms)
-    grouped = grouped.transpose(0, 2, 4, 1, 3, 5, 6).reshape(-1, 8, terms)
-    return jnp.einsum("pok,oak->pa", grouped, operators, precision=lax.Precision.HIGHEST)
 
 
 def per_device(
@@ -421,33 +546,10 @@
     live_mask = (slot_of[None, None, :] < jnp.repeat(counts, SLOTS, axis=2)).astype(F32)
     weights = charges * live_mask
     stacked = jnp.concatenate([positions, weights[None]], axis=0)
-    column_halo = padded(stacked, (("gz", 3),), SLOTS)
-    extended = padded(column_halo, (("gx", 1), ("gy", 2)), 1)
     order = jnp.asarray(permutation(*sizes))
     vmem = pl.BlockSpec(memory_space=pltpu.VMEM)
     smem = pl.BlockSpec(memory_space=pltpu.SMEM)
-    leaf, mid, upper = pl.pallas_call(
-        lambda *refs: moment_kernel(block_z, *refs),
-        out_shape=(
-            jax.ShapeDtypeStruct((leaves, LANES), F32),
-            jax.ShapeDtypeStruct((leaves // 8, LANES), F32),
-            jax.ShapeDtypeStruct((8, LANES), F32),
-        ),
-        in_specs=[vmem] * 3,
-        out_specs=(vmem, vmem, vmem),
-        scratch_shapes=[pltpu.VMEM(((padded_terms + 1) * columns, column), F32)],
-        name="moments",
-    )(stacked.reshape(4, columns, column), moment_shift, order)
-    axes = (("gx", 0), ("gy", 1), ("gz", 2))
-    wide_leaf = padded(leaf.reshape(block_x, block_y, block_z, LANES), axes, 2)
-    wide_mid = padded(mid.reshape(block_x // 2, block_y // 2, block_z // 2, LANES), axes, 2)
-    wide_mid = jnp.pad(wide_mid, ((0, 0), (0, 0), (0, 8 - wide_mid.shape[2]), (0, 0)))
-    uppers = lax.all_gather(upper[:1], ("gx", "gy", "gz"), axis=0, tiled=True)
-    tops = moments_merge(
-        uppers[:, :terms].reshape(number_x, number_y, number_z, terms), moment_shift.astype(F32)
-    )
-    root = jnp.sum(tops, axis=0, keepdims=True)
-    top_count = tops.shape[0]
+    top_count = number_x * number_y * number_z // 8
     top_sizes = (number_x // 2, number_y // 2, number_z // 2)
     shifts = offset_table()
     offsets = shifts.shape[0]
@@ -475,21 +577,14 @@
                 entries + (moved[0] * top_sizes[1] + moved[1]) * top_sizes[2] + moved[2]
             )
     index = jnp.where(jnp.arange(upper_rows)[None, :] == 0, picked[:, None], jnp.asarray(static))
-    table = jnp.concatenate([uppers[:, :terms], tops], axis=0)
-    table = jnp.pad(table, ((0, 0), (0, LANES - terms)))
-    rounded = lax.reduce_precision(table, 8, 7)
-    both = jnp.concatenate([rounded, lax.reduce_precision(table - rounded, 8, 7)], axis=1)
-    chosen = (index[:, :, None] == jnp.arange(entries + top_count)[None, None, :]).astype(BF16)
-    upper_table = jnp.dot(
-        chosen.reshape(offsets * upper_rows, -1), both.astype(BF16), preferred_element_type=F32
-    ).reshape(offsets, upper_rows, 2 * LANES)
+    chosen = (index[:, :, None] == jnp.arange(entries + top_count)[None, None, :]).astype(F32)
     parent = (index_x // 2 * top_sizes[1] + index_y // 2) * top_sizes[2] + index_z // 2
     octant = index_x % 2 * 4 + index_y % 2 * 2 + index_z % 2
     where = jnp.stack([parent, octant]).astype(jnp.int32)
     wide_x, wide_y = block_x + 5, block_y + 5
     half_x, half_y = block_x // 2, block_y // 2
     potential, field_out = pl.pallas_call(
-        lambda *refs: field_kernel(sizes, top_count, *refs),
+        lambda *refs: field_kernel(sizes, numbers, *refs),
         out_shape=(
             jax.ShapeDtypeStruct((columns, column), F32),
             jax.ShapeDtypeStruct((3, columns, column), F32),
@@ -497,6 +592,12 @@
         in_specs=[smem, smem] + [vmem] * 10,
         out_specs=(vmem, vmem),
         scratch_shapes=[
+            pltpu.VMEM((3, block_x + 2, block_y + 2, 4, column), F32),
+            pltpu.VMEM((3, block_x + 4, block_y + 4, block_z, LANES), F32),
+            pltpu.VMEM((3, half_x + 4, half_y + 4, block_z // 2, LANES), F32),
+            pltpu.VMEM((entries * 8 + 8, LANES), F32),
+            pltpu.VMEM((leaves, LANES), F32),
+            pltpu.VMEM((offsets, upper_rows, 2 * LANES), F32),
             pltpu.VMEM((36, (block_x + 4) * block_y, column), F32),
             pltpu.VMEM((7, block_x + 4 + block_x, block_y + 4 + block_y, 8, LANES), F32),
             pltpu.VMEM((7, half_x + 4 + half_x, half_y + 4 + half_y, 8, LANES), F32),
@@ -504,22 +605,28 @@
             pltpu.VMEM((upper_rows, terms), F32),
             pltpu.VMEM(((padded_terms + 1) * columns, column), F32),
             pltpu.VMEM((columns * 8 + half_x * half_y * 8 + 2 * upper_rows, padded_terms), F32),
+            pltpu.SemaphoreType.DMA((3, 27)),
+            pltpu.SemaphoreType.DMA((3, 27)),
+            pltpu.SemaphoreType.DMA((entries,)),
+            pltpu.SemaphoreType.DMA((entries,)),
         ],
-        compiler_params=pltpu.CompilerParams(vmem_limit_bytes=60 * 1024 * 1024),
+        compiler_params=pltpu.CompilerParams(
+            vmem_limit_bytes=60 * 1024 * 1024, collective_id=0, has_side_effects=True
+        ),
         name="fields",
     )(
         jnp.asarray(plan_table(block_x, block_y)),
         where,
-        extended,
+        jnp.transpose(stacked, (1, 2, 0, 3)),
+        stacked.reshape(4, columns, column),
         live_mask.reshape(columns, column),
-        wide_leaf,
-        wide_mid,
-        upper_table,
-        root,
+        moment_shift,
         far_operators,
         local_shift,
         lattice_operator,
         order,
+        jnp.asarray(permutation(*numbers)),
+        chosen,
     )
     return (
         potential.reshape(block_x, block_y, column),

time: 214 us -> 94.1 us (0.44)
  blocking collectives: 65.7 us -> 0 us
  starting transfers between devices: 20.8 us -> 0 us
  Pallas kernels: 103 us -> 82.7 us
  waiting for transfers between devices: 5.89 us -> 0 us
  matrix products: 3.82 us -> 0 us
  other arithmetic: 8.63 us -> 6.03 us
    all_gather x1 -> x0, blocking collectives: 65.7 us -> none  [per_device(): uppers = lax.all_gather(upper[:1], ('gx', 'gy', 'gz'), axis=0, tiled=True)]
    ppermute x18 -> x0, starting transfers between devices: 20.8 us -> none  [the longest x9 12.7 us: padded(): lax.ppermute(head, axis, [((i + 1) % count, i) for i in range(count)])]
    pallas_call x2 -> x1, Pallas kernels: 103 us -> 82.7 us  [per_device(): pl.pallas_call(lambda *refs: field_kernel(sizes, numbers, *refs), out_sha...]
    ppermute x18 -> x0, waiting for transfers between devices: 5.89 us -> none  [the longest x9 3.78 us: padded(): lax.ppermute(tail, axis, [(i, (i + 1) % count) for i in range(count)])]
    dot_general x2 -> x0, matrix products: 3.82 us -> none  [the longest x1 2.15 us: per_device(): jnp.dot(chosen.reshape(offsets * upper_rows, -1), both.astype(BF16), pref...]
    concatenate x7 -> x0, other arithmetic: 2.42 us -> none  [padded(): jnp.concatenate([lax.ppermute(tail, axis, [(i, (i + 1) % count) for i in...]
  transfers between devices with their start and end apart: 18 -> 0, of which waited for: 4 -> 0; matrix products, arithmetic and copies ran while one was open for 6% -> 0% of each run, Pallas kernels for 0% -> 0%
where the time goes in v1:
time: 94.1 us; the launch traced here: 93.8 us
  Pallas kernels  82.7 us (88%)
  other arithmetic  6.03 us (6%)
  local copies, waits for them, and re-layouts  4.33 us (5%)
    pallas_call x1, Pallas kernels, per_device(): pl.pallas_call(lambda *refs: field_kernel(sizes, numbers, *refs), out_sha...  82.7 us
    unnamed x15, local copies, waits for them, and re-layouts  4.08 us

profile of v1, /device:TPU:0, one launch (start us, length us, event | category | flops | bytes accessed | tf_op | source)
XLA Modules:
  0.0 93.8 jit_solution(11321079522910451015)
XLA Ops:
  0.6 0.0 copy-start.3
  0.6 0.0 copy-start.4
  0.7 0.0 copy-start.2
  0.7 0.0 copy-start
  0.7 0.0 copy-start.1
  0.7 0.8 fusion.5
  1.5 1.0 %broadcast_select_fusion = s32[316,8]{1,0:T(8,128)S(1)} fusion(s32[316,8]{1,0:T(8,128)} %constant.130.clone, s32[316]{0:T(512)S(1)} %fusion.5, pred[8]{0:T(512)(128)(4,1)S(1)} %iota_compare_fusion.1), kind=kLoop, calls=%fused_computation.2 | loop fusion | flops 2528 | bytes 21496 | tf_op jit(solution)/shard_map/jit(_where)/select_n | solution.py:579
  2.6 1.7 %fusion.refs_11_ = f32[316,8,36]{2,1,0:T(8,128)} fusion(s32[316,8]{1,0:T(8,128)S(1)} %broadcast_select_fusion), kind=kLoop, calls=%fused_computation.1 | loop fusion | flops 182016 | bytes 374144 | tf_op jit(solution)/shard_map/convert_element_type | solution.py:580
  4.2 0.7 pad_add_fusion.refs_1_
  4.9 0.0 copy-done.3
  4.9 0.1 broadcast_in_dim.31
  5.0 0.1 reshape.37
  5.1 0.0 copy-done.4
  5.1 0.0 copy-done.2
  5.1 0.6 maximum_bitcast_fusion.refs_2_
  5.8 0.6 pad_maximum_fusion.refs_3_
  6.4 0.1 reshape.38
  6.5 0.6 compare_convert_fusion.refs_4_
  7.1 0.0 copy-done
  7.1 0.7 copy.23.refs_5_
  7.8 0.0 copy-done.1
  7.8 0.7 copy.24.refs_7_
  8.5 82.7 %fields.1 = (f32[16,128]{1,0:T(8,128)}, f32[3,16,128]{2,1,0:T(8,128)}) custom-call(s32[5056]{0:T(1024)} %constant.131.clone.refs_0_, s32[2]{0:T(128)} %pad_add_fusion.refs_1_, f32[4,4,4,128]{3,2,1,0:T(4,128)} %maximum_bitcast_fusion.refs_2_, f32[4,16,128]{2,1,0:T(8,128)} %pad_maximum_fusion.refs_3_, f32[16,128]{1,0:T(8,128)} %compare_convert_fusion.refs_4_, ...), custom_call_target="tpu_custom_call" | custom-call | tf_op jit(solution)/shard_map/fields/pallas_call | solution.py:586
  91.2 1.3 %copy.27 = f32[4,4,128]{2,1,0:T(4,128)} copy(f32[4,4,128]{2,1,0:T(4,128)} %bitcast.13) | data formatting | bytes 16384
  92.5 1.3 %copy.28 = f32[3,4,4,128]{3,2,1,0:T(4,128)} copy(f32[3,4,4,128]{3,2,1,0:T(4,128)} %bitcast.12) | data formatting | bytes 49152
  (4 shorter events, 0.0 us)
Async XLA Ops:
  0.6 4.3 %copy-start.3 = (s32[4,4,4]{2,1,0:T(4,128)S(1)}, s32[4,4,4]{2,1,0:T(4,128)}, u32[]{:S(2)}) copy-start(s32[4,4,4]{2,1,0:T(4,128)} %param.22) | copy-start | bytes 772
  0.6 4.4 %copy-start.4 = (f32[4,4,128]{2,1,0:T(4,128)S(1)}, f32[4,4,128]{2,1,0:T(4,128)}, u32[]{:S(2)}) copy-start(f32[4,4,128]{2,1,0:T(4,128)} %param.21) | copy-start | bytes 24580
  0.7 4.4 %copy-start.2 = (f32[3,4,4,128]{3,2,1,0:T(4,128)S(1)}, f32[3,4,4,128]{3,2,1,0:T(4,128)}, u32[]{:S(2)}) copy-start(f32[3,4,4,128]{3,2,1,0:T(4,128)} %param.20) | copy-start | bytes 73732
  0.7 6.4 %copy-start = (bf16[8,81,81]{2,0,1:T(8,128)(2,1)S(1)}, bf16[8,81,81]{2,0,1:T(8,128)(2,1)}, u32[]{:S(2)}) copy-start(bf16[8,81,81]{2,0,1:T(8,128)(2,1)} %param.23) | copy-start | bytes 314932
  0.7 7.1 %copy-start.1 = (bf16[8,81,81]{2,0,1:T(8,128)(2,1)S(1)}, bf16[8,81,81]{2,0,1:T(8,128)(2,1)}, u32[]{:S(2)}) copy-start(bf16[8,81,81]{2,0,1:T(8,128)(2,1)} %param.25) | copy-start | bytes 314932

commit v2 on v1

--- a/solution.py
+++ b/solution.py
@@ -281,25 +281,26 @@
 
     def place(row, carry):
         start = row * terms
-        base = jnp.minimum(start // LANES * LANES, far_ref.shape[1] - 2 * LANES)
+        base = jnp.minimum(start & -LANES, far_ref.shape[1] - 2 * LANES)
         base = pl.multiple_of(base, LANES)
         held = far_ref[:, pl.ds(base, 2 * LANES)].astype(F32)
         held = jnp.concatenate(
             [held, jnp.zeros((padded_terms - terms, 2 * LANES), F32)], axis=0
         )
-        turned = pltpu.roll(held, lax.rem(2 * LANES - (start - base), 2 * LANES), 1)
+        turned = pltpu.roll(held, (2 * LANES - (start - base)) & (2 * LANES - 1), 1)
         return turned[:, :LANES].astype(BF16)
 
     def place_pair(pair, carry):
-        operators[pair, :, :LANES] = place(2 * pair, carry)
-        operators[pair, :, LANES:] = place(2 * pair + 1, carry)
-        return carry
-
-    lax.fori_loop(0, offsets // 2, place_pair, 0, unroll=2)
+        for which in range(2):
+            operators[2 * pair + which, :, :LANES] = place(4 * pair + 2 * which, carry)
+            operators[2 * pair + which, :, LANES:] = place(4 * pair + 2 * which + 1, carry)
+        return carry
+
+    lax.fori_loop(0, offsets // 4, place_pair, 0)
 
     lane = lax.broadcasted_iota(jnp.int32, (columns, width), 1)
     group = lane - lane % SLOTS
-    turns = [group + (lane + step) % SLOTS for step in range(1, 5)]
+    turns = [group + (lane + step) % SLOTS for step in range(1, 9)]
     target_x = data_ref[0]
     target_y = data_ref[1]
     target_z = data_ref[2]
@@ -350,7 +351,7 @@
             held, totals = carry
             keep = jnp.where(own & (at == 0), 0.0, 1.0)
             sum_p, sum_x, sum_y, sum_z = totals
-            for turn in range(4):
+            for turn in range(8):
                 if turn == 0:
                     s_x, s_y, s_z, s_q = held
                     s_q = s_q * keep
@@ -368,10 +369,10 @@
                 sum_x = sum_x + cubic * d_x
                 sum_y = sum_y + cubic * d_y
                 sum_z = sum_z + cubic * d_z
-            held = tuple(jnp.take_along_axis(value, turns[3], axis=1) for value in held)
+            held = tuple(jnp.take_along_axis(value, turns[7], axis=1) for value in held)
             return held, (sum_p, sum_x, sum_y, sum_z)
 
-        return lax.fori_loop(0, SLOTS // 4, step, (source, totals))[1]
+        return lax.fori_loop(0, SLOTS // 8, step, (source, totals))[1]
 
     zero = jnp.zeros((columns, width), F32)
     near = lax.fori_loop(0, 27, neighbour, (zero, zero, zero, zero))
@@ -460,14 +461,20 @@
         return jnp.concatenate(pieces, axis=0).astype(BF16)
 
     def far_step(pair, total):
-        left = jnp.concatenate([gathered(2 * pair), gathered(2 * pair + 1)], axis=1)
-        return total + lax.dot_general(left, operators[pair], NT, preferred_element_type=F32)
+        added = []
+        for which in range(2):
+            row = 4 * pair + 2 * which
+            left = jnp.concatenate([gathered(row), gathered(row + 1)], axis=1)
+            added.append(
+                lax.dot_general(left, operators[2 * pair + which], NT, preferred_element_type=F32)
+            )
+        return total + (added[0] + added[1])
 
     leaf_count = columns * 8
     mid_count = half_x * half_y * 8
     total_rows = leaf_count + mid_count + 2 * upper_rows
     sums[...] = lax.fori_loop(
-        0, offsets // 2, far_step, jnp.zeros((total_rows, padded_terms), F32), unroll=2
+        0, offsets // 4, far_step, jnp.zeros((total_rows, padded_terms), F32)
     )
     first = leaf_count + mid_count
     far_high = sums[first : first + upper_rows, :terms] + sums[first + upper_rows :, :terms]

time: 94.1 us -> 86.3 us (0.917)
  Pallas kernels: 82.7 us -> 75 us
    pallas_call x1, Pallas kernels: 82.7 us -> 75 us  [per_device(): pl.pallas_call(lambda *refs: field_kernel(sizes, numbers, *refs), out_sha...]
where the time goes in v2:
time: 86.3 us; the launch traced here: 86.1 us
  Pallas kernels  75 us (87%)
  other arithmetic  6.03 us (7%)
  local copies, waits for them, and re-layouts  4.33 us (5%)
    pallas_call x1, Pallas kernels, per_device(): pl.pallas_call(lambda *refs: field_kernel(sizes, numbers, *refs), out_sha...  75 us
    unnamed x15, local copies, waits for them, and re-layouts  4.08 us

profile of v2, /device:TPU:0, one launch (start us, length us, event | category | flops | bytes accessed | tf_op | source)
XLA Modules:
  0.0 86.1 jit_solution(4853445425425897028)
XLA Ops:
  0.6 0.0 copy-start.3
  0.6 0.0 copy-start.4
  0.7 0.0 copy-start.2
  0.7 0.0 copy-start
  0.7 0.0 copy-start.1
  0.7 0.8 fusion.5
  1.5 1.0 %broadcast_select_fusion = s32[316,8]{1,0:T(8,128)S(1)} fusion(s32[316,8]{1,0:T(8,128)} %constant.130.clone, s32[316]{0:T(512)S(1)} %fusion.5, pred[8]{0:T(512)(128)(4,1)S(1)} %iota_compare_fusion.1), kind=kLoop, calls=%fused_computation.2 | loop fusion | flops 2528 | bytes 21496 | tf_op jit(solution)/shard_map/jit(_where)/select_n | solution.py:586
  2.6 1.7 %fusion.refs_11_ = f32[316,8,36]{2,1,0:T(8,128)} fusion(s32[316,8]{1,0:T(8,128)S(1)} %broadcast_select_fusion), kind=kLoop, calls=%fused_computation.1 | loop fusion | flops 182016 | bytes 374144 | tf_op jit(solution)/shard_map/convert_element_type | solution.py:587
  4.2 0.7 pad_add_fusion.refs_1_
  4.9 0.0 copy-done.3
  4.9 0.1 broadcast_in_dim.31
  5.0 0.1 reshape.37
  5.1 0.0 copy-done.4
  5.1 0.0 copy-done.2
  5.1 0.6 maximum_bitcast_fusion.refs_2_
  5.8 0.6 pad_maximum_fusion.refs_3_
  6.4 0.1 reshape.38
  6.5 0.6 compare_convert_fusion.refs_4_
  7.1 0.0 copy-done
  7.1 0.7 copy.23.refs_5_
  7.8 0.0 copy-done.1
  7.8 0.7 copy.24.refs_7_
  8.5 75.0 %fields.1 = (f32[16,128]{1,0:T(8,128)}, f32[3,16,128]{2,1,0:T(8,128)}) custom-call(s32[5056]{0:T(1024)} %constant.131.clone.refs_0_, s32[2]{0:T(128)} %pad_add_fusion.refs_1_, f32[4,4,4,128]{3,2,1,0:T(4,128)} %maximum_bitcast_fusion.refs_2_, f32[4,16,128]{2,1,0:T(8,128)} %pad_maximum_fusion.refs_3_, f32[16,128]{1,0:T(8,128)} %compare_convert_fusion.refs_4_, ...), custom_call_target="tpu_custom_call" | custom-call | tf_op jit(solution)/shard_map/fields/pallas_call | solution.py:593
  83.5 1.3 %copy.27 = f32[4,4,128]{2,1,0:T(4,128)} copy(f32[4,4,128]{2,1,0:T(4,128)} %bitcast.13) | data formatting | bytes 16384
  84.8 1.3 %copy.28 = f32[3,4,4,128]{3,2,1,0:T(4,128)} copy(f32[3,4,4,128]{3,2,1,0:T(4,128)} %bitcast.12) | data formatting | bytes 49152
  (4 shorter events, 0.0 us)
Async XLA Ops:
  0.6 4.3 %copy-start.3 = (s32[4,4,4]{2,1,0:T(4,128)S(1)}, s32[4,4,4]{2,1,0:T(4,128)}, u32[]{:S(2)}) copy-start(s32[4,4,4]{2,1,0:T(4,128)} %param.22) | copy-start | bytes 772
  0.6 4.4 %copy-start.4 = (f32[4,4,128]{2,1,0:T(4,128)S(1)}, f32[4,4,128]{2,1,0:T(4,128)}, u32[]{:S(2)}) copy-start(f32[4,4,128]{2,1,0:T(4,128)} %param.21) | copy-start | bytes 24580
  0.7 4.4 %copy-start.2 = (f32[3,4,4,128]{3,2,1,0:T(4,128)S(1)}, f32[3,4,4,128]{3,2,1,0:T(4,128)}, u32[]{:S(2)}) copy-start(f32[3,4,4,128]{3,2,1,0:T(4,128)} %param.20) | copy-start | bytes 73732
  0.7 6.4 %copy-start = (bf16[8,81,81]{2,0,1:T(8,128)(2,1)S(1)}, bf16[8,81,81]{2,0,1:T(8,128)(2,1)}, u32[]{:S(2)}) copy-start(bf16[8,81,81]{2,0,1:T(8,128)(2,1)} %param.23) | copy-start | bytes 314932
  0.7 7.1 %copy-start.1 = (bf16[8,81,81]{2,0,1:T(8,128)(2,1)S(1)}, bf16[8,81,81]{2,0,1:T(8,128)(2,1)}, u32[]{:S(2)}) copy-start(bf16[8,81,81]{2,0,1:T(8,128)(2,1)} %param.25) | copy-start | bytes 314932
